TPU v7x, 512 devices: a whole 4x8x8 slice. The times are simulated.
512 devices in a mesh: gx: 64 (over z, x, core), ta: 8 (over y).
Axes of the slice: x: 4, y: 8, z: 8, core: 2. Of those that a mesh axis runs over, the one named last changes fastest.
Arguments:
- d_out: bfloat16 [16384, 4096], P('gx', 'ta'), may hold values from -0.75 to 0.75
- kept: int32 [2048], P('gx'), may hold values from 0 to 16383, as said below
- expert_ids: int32 [2048, 8], P('gx'), may hold values from 0 to 63, all different within a row; in each aligned block of 32 rows (0 to 31, 32 to 63, ...) at most 8 rows name the same one
- gates: bfloat16 [2048, 8], P('gx'), may hold values from 0.049804688 to 1
- down_weight: bfloat16 [64, 1536, 4096], P('gx', 'ta'), may hold values from -0.15625 to 0.15625
- gate_pre: bfloat16 [64, 1536, 512], P('gx', 'ta'), may hold values from -6 to 6
- up_pre: bfloat16 [64, 1536, 512], P('gx', 'ta'), may hold values from -6 to 6
- query: bfloat16 [2048, 8192], P('gx', 'ta'), may hold values from -6 to 6
- keys: bfloat16 [2048, 512], P('gx'), may hold values from -6 to 6
- values: bfloat16 [2048, 512], P('gx'), may hold values from -6 to 6
- d_attn: bfloat16 [2048, 8192], P('gx', 'ta'), may hold values from -12 to 12
Outputs:
- d_down: bfloat16 [64, 1536, 4096], P('gx', 'ta')
- d_gate_pre: bfloat16 [64, 1536, 512], P('gx', 'ta')
- d_up_pre: bfloat16 [64, 1536, 512], P('gx', 'ta')
- d_gates: float32 [2048, 8], P('gx')
- d_query: bfloat16 [2048, 8192], P('gx', 'ta')
- d_key: float32 [2048, 512], P('gx')
- d_value: float32 [2048, 512], P('gx')
Inputs may be any that keep to these rules, and one draw needn't show every extreme that they name: `kept`: rising; the 32 selected tokens of block i lie in positions i * 256 to (i + 1) * 256 - 1 and include both ends. `expert_ids`: each row names 8 different experts; in each aligned block of 32 rows no expert is named more than 8 times.
All inputs are finite; a program needn't handle non-finite values.
Results may differ from a plain program's by a relative error of at most 0.0068.
Values may be sent and summed in bfloat16 or wider, within the bound.
No kernel may reach another device: no remote copies, remote signals or barrier semaphores. Data moves between devices by JAX's collectives and lax.ppermute only.
A program may use at most 64 MiB of HBM per device.

v0:
```python
import jax
import jax.numpy as jnp
from jax import lax
from jax.sharding import PartitionSpec as P

H = 64
KVH = 4
HD = 128


def on_device(
    d_out, kept, expert_ids, gates, down_weight, gate_pre, up_pre, query, keys, values, d_attn
):
    n_experts = lax.axis_size("gx")
    keep_dev = kept.shape[0]
    tok_dev = d_out.shape[0]
    top = expert_ids.shape[1]
    slot_count = gate_pre.shape[2]
    cap = slot_count // n_experts
    picked = jnp.take(d_out, kept % tok_dev, axis=0)
    flat_ids = expert_ids.reshape(-1)
    onehot = (flat_ids[:, None] == jnp.arange(n_experts, dtype=jnp.int32)[None, :]).astype(
        jnp.int32
    )
    rank = jnp.sum((jnp.cumsum(onehot, axis=0) - onehot) * onehot, axis=1)
    dest = flat_ids * cap + rank
    match = dest[:, None] == jnp.arange(slot_count, dtype=jnp.int32)[None, :]
    match_rows = jnp.sum(
        match.reshape(keep_dev, top, slot_count).astype(jnp.float32), axis=1
    ).astype(jnp.bfloat16)
    gate_slots = jnp.sum(jnp.where(match, gates.reshape(-1, 1).astype(jnp.float32), 0.0), axis=0)
    gate_slots = gate_slots.astype(jnp.bfloat16).reshape(n_experts, cap)
    full_rows = lax.all_gather(picked, "ta", axis=1, tiled=True)
    packed = lax.dot_general(
        match_rows, full_rows, (((0,), (0,)), ((), ())), preferred_element_type=jnp.float32
    )
    arrived = lax.all_to_all(
        packed.astype(jnp.bfloat16).reshape(n_experts, cap, full_rows.shape[1]),
        "gx",
        split_axis=0,
        concat_axis=0,
        tiled=True,
    )
    arrived_gates = lax.all_to_all(gate_slots, "gx", split_axis=0, concat_axis=0, tiled=True)
    slot_rows = arrived.reshape(slot_count, -1)
    slot_weight = arrived_gates.reshape(-1).astype(jnp.float32)
    weight = down_weight[0]
    z = lax.dot_general(
        weight, slot_rows, (((1,), (1,)), ((), ())), preferred_element_type=jnp.float32
    )
    g = gate_pre[0].astype(jnp.float32)
    u = up_pre[0].astype(jnp.float32)
    sig = jax.nn.sigmoid(g)
    act = g * sig
    hidden = act * u
    slot_dots = jnp.sum(hidden * z, axis=0)
    grad_hidden = z * slot_weight[None, :]
    grad_up = (grad_hidden * act).astype(jnp.bfloat16)[None]
    grad_gate = (grad_hidden * u * sig * (1.0 + g * (1.0 - sig))).astype(jnp.bfloat16)[None]
    weighted = (hidden * slot_weight[None, :]).astype(jnp.bfloat16)
    grad_weight = jnp.dot(weighted, slot_rows, preferred_element_type=jnp.float32).astype(
        jnp.bfloat16
    )[None]
    returned = lax.all_to_all(
        slot_dots.reshape(n_experts, cap), "gx", split_axis=0, concat_axis=0, tiled=True
    )
    gate_terms = jnp.sum(jnp.where(match, returned.reshape(1, -1), 0.0), axis=1).reshape(
        keep_dev, top
    )
    local_heads = query.shape[1] // HD
    group = H // KVH
    kv_local = max(1, local_heads // group)
    per_kv = local_heads // kv_local
    first_kv = lax.axis_index("ta") * local_heads // group
    key_local = lax.dynamic_slice_in_dim(keys, first_kv * HD, kv_local * HD, 1)
    value_local = lax.dynamic_slice_in_dim(values, first_kv * HD, kv_local * HD, 1)
    key_all, value_all = (
        lax.all_gather(key_local, "gx", axis=0, tiled=True),
        lax.all_gather(value_local, "gx", axis=0, tiled=True),
    )
    total = key_all.shape[0]
    key_three = key_all.reshape(total, kv_local, HD)
    value_three = value_all.reshape(total, kv_local, HD)
    query_four = query.reshape(keep_dev, kv_local, per_kv, HD)
    grad_four = d_attn.reshape(keep_dev, kv_local, per_kv, HD)
    scale = HD ** (-0.5)
    scores = (
        jnp.einsum("qcgd,kcd->cgqk", query_four, key_three, preferred_element_type=jnp.float32)
        * scale
    )
    query_pos = lax.axis_index("gx") * keep_dev + jnp.arange(keep_dev)
    causal = jnp.arange(total)[None, :] <= query_pos[:, None]
    scores = jnp.where(causal[None, None], scores, -1e30)
    top_score = jnp.max(scores, axis=3, keepdims=True)
    expo = jnp.exp(scores - top_score)
    probs = expo / jnp.sum(expo, axis=3, keepdims=True)
    grad_probs = jnp.einsum(
        "qcgd,kcd->cgqk", grad_four, value_three, preferred_element_type=jnp.float32
    )
    grad_scores = probs * (grad_probs - jnp.sum(probs * grad_probs, axis=3, keepdims=True))
    probs_b = probs.astype(jnp.bfloat16)
    grad_b = grad_scores.astype(jnp.bfloat16)
    grad_query = (
        jnp.einsum("cgqk,kcd->qcgd", grad_b, key_three, preferred_element_type=jnp.float32) * scale
    )
    grad_query = grad_query.astype(jnp.bfloat16).reshape(keep_dev, -1)
    key_part = (
        jnp.einsum("cgqk,qcgd->kcd", grad_b, query_four, preferred_element_type=jnp.float32) * scale
    )
    value_part = jnp.einsum(
        "cgqk,qcgd->kcd", probs_b, grad_four, preferred_element_type=jnp.float32
    )
    owned = lax.psum_scatter(
        jnp.concatenate(
            [
                key_part.reshape(keep_dev * lax.axis_size("gx"), -1),
                value_part.reshape(keep_dev * lax.axis_size("gx"), -1),
            ],
            axis=1,
        ),
        "gx",
        scatter_dimension=0,
        tiled=True,
    )
    width = kv_local * HD
    empty = jnp.zeros((keep_dev, KVH * HD), jnp.float32)
    key_full = lax.dynamic_update_slice(empty, owned[:, :width], (0, first_kv * HD))
    value_full = lax.dynamic_update_slice(empty, owned[:, width:], (0, first_kv * HD))
    grad_gates, grad_key, grad_value = lax.psum((gate_terms, key_full, value_full), "ta")
    return (grad_weight, grad_gate, grad_up, grad_gates, grad_query, grad_key, grad_value)


def solution(mesh):
    in_specs = (
        P("gx", "ta"),
        P("gx"),
        P("gx", None),
        P("gx", None),
        P("gx", "ta", None),
        P("gx", "ta", None),
        P("gx", "ta", None),
        P("gx", "ta"),
        P("gx", None),
        P("gx", None),
        P("gx", "ta"),
    )
    out_specs = (
        P("gx", "ta", None),
        P("gx", "ta", None),
        P("gx", "ta", None),
        P("gx", None),
        P("gx", "ta"),
        P("gx", None),
        P("gx", None),
    )
    return jax.shard_map(
        on_device, mesh=mesh, in_specs=in_specs, out_specs=out_specs, check_vma=False
    )
```

profile of v0, /device:TPU:2, one launch (start us, length us, event | category | flops | bytes accessed | tf_op | source)
XLA Modules:
  0.0 499.3 jit_solution(1224681247285578095)
XLA Ops:
  7.2 0.0 copy-start
  7.2 0.9 copy.53
  8.1 0.1 reshape.204
  8.2 0.0 copy-start.6
  8.2 0.1 eq.48
  8.2 0.7 compare_and_fusion
  8.9 1.6 gather_fusion
  10.6 0.1 broadcast_select_fusion
  10.6 26.4 %all_gather.9 = bf16[32,4096]{1,0:T(8,128)(2,1)S(1)} all-gather(bf16[32,512]{1,0:T(8,128)(2,1)S(1)} %broadcast_select_fusion), channel_id=1, replica_groups=mesh['gx'=64,'ta'=8] {'ta'}, dimensions={1}, use_global_device_ids=true | all-gather | bytes 294912 | tf_op jit(solution)/shard_map/all_gather | solution.py:33
  37.0 0.6 reduce-window.6
  37.6 0.2 slice_reduce_fusion
  37.8 0.1 fusion.50
  38.0 0.1 reduce_sum.67
  38.1 0.2 convert_reduce_fusion
  38.3 3.2 fusion
  41.6 14.2 %all-to-all-start.1 = ((bf16[64,8,4096]{2,1,0:T(8,128)(2,1)}), bf16[64,8,4096]{2,1,0:T(8,128)(2,1)}, u32[]{:S(2)}, u32[]{:S(2)}) async-start(bf16[64,8,4096]{2,1,0:T(8,128)(2,1)} %fusion), calls=%async_computation.1 | async-start | bytes 8388608 | tf_op jit(solution)/shard_map/all_to_all | solution.py:37
  55.8 0.0 reduce-scatter.4.cloned.1.call-start
  55.8 0.7 constant_dynamic-slice_fusion.1
  56.5 0.7 constant_dynamic-slice_fusion
  57.2 134.0 %all_gather.10 = bf16[2048,128]{1,0:T(8,128)(2,1)S(1)} all-gather(bf16[32,128]{1,0:T(8,128)(2,1)S(1)} %constant_dynamic-slice_fusion.1), channel_id=1, replica_groups=mesh['gx'=64,'ta'=8] {'gx'}, dimensions={0}, use_global_device_ids=true | all-gather | bytes 532480 | tf_op jit(solution)/shard_map/all_gather | solution.py:78
  191.3 48.7 %all_gather.11 = bf16[2048,128]{1,0:T(8,128)(2,1)S(1)} all-gather(bf16[32,128]{1,0:T(8,128)(2,1)S(1)} %constant_dynamic-slice_fusion), channel_id=1, replica_groups=mesh['gx'=64,'ta'=8] {'gx'}, dimensions={0}, use_global_device_ids=true | all-gather | bytes 532480 | tf_op jit(solution)/shard_map/all_gather | solution.py:79
  240.0 0.1 iota_compare_fusion.2
  240.1 0.5 fusion.64
  240.7 0.0 copy-start.11
  240.7 0.4 fusion.9
  241.1 0.4 copy-done.11
  241.5 0.6 multiply_reduce_fusion
  242.2 0.6 fusion.18
  242.8 0.4 fusion.7
  243.2 0.6 convolution_bitcast_fusion.1
  243.8 1.4 pad_maximum_fusion
  245.2 3.0 copy.68
  248.2 0.0 reduce-scatter.4.cloned.1.call-update
  248.2 0.8 copy.56
  249.0 0.7 reshape.214
  249.7 0.4 fusion.17
  250.1 0.6 copy.98
  250.8 0.0 copy-start.10
  250.8 0.0 all-to-all-done.1
  250.8 3.8 fusion.33
  254.6 0.7 all_to_all.15
  255.3 8.7 %all-to-all-start.2 = ((f32[64,1,8]{2,1,0:T(1,128)}), f32[64,1,8]{2,1,0:T(1,128)S(1)}, u32[]{:S(2)}, u32[]{:S(2)}) async-start(f32[64,1,8]{2,1,0:T(1,128)} %bitcast.11), calls=%async_computation.2 | async-start | bytes 65536 | tf_op jit(solution)/shard_map/all_to_all | solution.py:64
  264.0 132.1 %reduce-scatter.4.cloned.1.call-done = f32[32,256]{1,0:T(8,128)} async-done(((f32[2048,256]{1,0:T(8,128)}), f32[32,256]{1,0:T(8,128)}) %reduce-scatter.4.cloned.1.call-update) | async-done | bytes 32784
  396.1 0.7 slice_dynamic-update-slice_fusion.1
  396.9 0.5 broadcast.112
  397.4 0.7 reduce.12
  398.1 0.1 broadcast_in_dim.79
  398.2 0.2 select_reduce_fusion
  398.5 0.7 convert_element_type.130
  399.2 8.1 %all-to-all-start = ((bf16[64,1,8]{2,1,0:T(2,128)(2,1)}), bf16[64,1,8]{2,1,0:T(2,128)(2,1)S(1)}, u32[]{:S(2)}, u32[]{:S(2)}) async-start(bf16[64,1,8]{2,1,0:T(2,128)(2,1)} %convert_element_type.130), calls=%async_computation | async-start | bytes 65536 | tf_op jit(solution)/shard_map/all_to_all | solution.py:44
  407.3 0.0 all-reduce.3.cloned.1.call-start
  407.4 0.7 slice_dynamic-update-slice_fusion
  408.1 0.6 copy-done.2
  408.7 0.0 all-reduce.3.cloned.1.call-update
  408.7 0.1 reshape.208
  408.8 29.7 %psum.21 = f32[32,8]{1,0:T(8,128)S(1)} all-reduce(f32[32,8]{1,0:T(8,128)S(1)} %reshape.208), channel_id=1, replica_groups=mesh['gx'=64,'ta'=8] {'ta'}, use_global_device_ids=true, to_apply=%region_7.8 | all-reduce | flops 256 | bytes 2048 | tf_op jit(solution)/shard_map/psum | solution.py:129
  438.5 0.7 copy.67
  439.2 0.1 convert_reduce_fusion.1
  439.3 0.1 reshape.215
  439.4 4.4 fusion.1
  443.8 0.9 fusion.43
  444.7 44.8 %all-reduce.3.cloned.1.call-done = (f32[32,512]{1,0:T(8,128)}, f32[32,512]{1,0:T(8,128)}) async-done(((f32[32,512]{1,0:T(8,128)}, f32[32,512]{1,0:T(8,128)}), (f32[32,512]{1,0:T(8,128)}, f32[32,512]{1,0:T(8,128)})) %all-reduce.3.cloned.1.call-update) | async-done | bytes 131088 | tf_op jit(solution)/shard_map/psum | solution.py:129
  489.5 1.5 copy.103
  491.0 1.5 copy.104
  (30 shorter events, 0.2 us)
Async XLA Ops:
  7.2 243.7 %copy-start = (bf16[1,192,4096]{2,1,0:T(8,128)(2,1)S(1)}, bf16[1,192,4096]{2,1,0:T(8,128)(2,1)}, u32[]{:S(2)}) copy-start(bf16[1,192,4096]{2,1,0:T(8,128)(2,1)} %param.15) | copy-start | bytes 4718596
  8.2 33.4 %copy-start.6 = (s32[256]{0:T(256)}, s32[256]{0:T(256)S(1)}, u32[]{:S(2)}) copy-start(s32[256]{0:T(256)S(1)} %reshape.204) | copy-start | bytes 3076
  38.0 3.6 copy-start.8
  41.6 198.6 %copy-start.1 = (bf16[32,1024]{1,0:T(8,128)(2,1)S(1)}, bf16[32,1024]{1,0:T(8,128)(2,1)}, u32[]{:S(2)}) copy-start(bf16[32,1024]{1,0:T(8,128)(2,1)} %param.18) | copy-start | bytes 196612
  41.6 209.3 %all-to-all-start.1 = ((bf16[64,8,4096]{2,1,0:T(8,128)(2,1)}), bf16[64,8,4096]{2,1,0:T(8,128)(2,1)}, u32[]{:S(2)}, u32[]{:S(2)}) async-start(bf16[64,8,4096]{2,1,0:T(8,128)(2,1)} %fusion), calls=%async_computation.1 | async-start | bytes 8388608 | tf_op jit(solution)/shard_map/all_to_all | solution.py:37
  55.8 340.4 %reduce-scatter.4.cloned.1.call-start = ((), (), s32[]{:S(2)}) async-start(), calls=%async_computation.4 | async-start | bytes 2129920
  240.7 0.8 copy-start.11
  248.2 2.7 copy-start.4
  248.2 2.7 copy-start.5
  249.7 1.1 copy-start.7
  249.7 1.1 copy-start.9
  250.8 147.4 %copy-start.10 = (f32[256]{0:T(256)S(1)}, f32[256]{0:T(256)}, u32[]{:S(2)}) copy-start(f32[256]{0:T(256)} %reshape.214) | copy-start | bytes 3076
  255.3 141.5 %all-to-all-start.2 = ((f32[64,1,8]{2,1,0:T(1,128)}), f32[64,1,8]{2,1,0:T(1,128)S(1)}, u32[]{:S(2)}, u32[]{:S(2)}) async-start(f32[64,1,8]{2,1,0:T(1,128)} %bitcast.11), calls=%async_computation.2 | async-start | bytes 65536 | tf_op jit(solution)/shard_map/all_to_all | solution.py:64
  396.8 11.2 %copy-start.3 = (f32[32,512]{1,0:T(8,128)}, f32[32,512]{1,0:T(8,128)S(1)}, u32[]{:S(2)}) copy-start(f32[32,512]{1,0:T(8,128)S(1)} %slice_dynamic-update-slice_fusion.1) | copy-start | bytes 196612
  399.2 40.0 %all-to-all-start = ((bf16[64,1,8]{2,1,0:T(2,128)(2,1)}), bf16[64,1,8]{2,1,0:T(2,128)(2,1)S(1)}, u32[]{:S(2)}, u32[]{:S(2)}) async-start(bf16[64,1,8]{2,1,0:T(2,128)(2,1)} %convert_element_type.130), calls=%async_computation | async-start | bytes 65536 | tf_op jit(solution)/shard_map/all_to_all | solution.py:44
  407.3 82.3 %all-reduce.3.cloned.1.call-start = ((), (), s32[]{:S(2)}) async-start(), calls=%async_computation.5 | async-start | bytes 262144 | tf_op jit(solution)/shard_map/psum | solution.py:129
  408.1 0.6 copy-start.2
Sparse Core Ops, SparseCore 0:
  248.3 147.7 reduce-scatter.3
  411.1 78.4 all-reduce.2
where the time goes:
time: 500 us; the launch traced here: 499 us
  blocking collectives  239 us (48%)
  waiting for transfers between devices  177 us (35%)
  starting transfers between devices  31 us (6%)
  local copies, waits for them, and re-layouts  17.8 us (4%)
  between operations  14.3 us (3%)
  matrix products  14 us (3%)
  other arithmetic  6.37 us (1%)
    all_gather x1, blocking collectives, on_device(): lax.all_gather(key_local, 'gx', axis=0, tiled=True)  134 us
    unnamed x3, waiting for transfers between devices  132 us
    all_gather x1, blocking collectives, on_device(): lax.all_gather(value_local, 'gx', axis=0, tiled=True)  48.7 us
    psum x1, waiting for transfers between devices, on_device(): lax.psum((gate_terms, key_full, value_full), 'ta')  44.8 us
    psum x1, blocking collectives, on_device(): lax.psum((gate_terms, key_full, value_full), 'ta')  29.7 us
    all_gather x1, blocking collectives, on_device(): full_rows = lax.all_gather(picked, 'ta', axis=1, tiled=True)  26.4 us
    all_to_all x1, starting transfers between devices, on_device(): lax.all_to_all(packed.astype(jnp.bfloat16).reshape(n_experts, cap, full_r...  14.2 us
  transfers between devices with their start and end apart: 5, of which 2 were waited for; matrix products, arithmetic and copies ran while one was open for 5% of the time, Pallas kernels for 0%

commit v1 on v0

--- a/solution.py
+++ b/solution.py
@@ -6,6 +6,11 @@
 H = 64
 KVH = 4
 HD = 128
+
+
+def exchange_gather(x, mesh_axis, d):
+    sent = jnp.stack([x] * lax.axis_size(mesh_axis))
+    return jnp.concatenate(lax.all_to_all(sent, mesh_axis, 0, 0), axis=d)
 
 
 def on_device(
@@ -75,7 +80,7 @@
     key_local = lax.dynamic_slice_in_dim(keys, first_kv * HD, kv_local * HD, 1)
     value_local = lax.dynamic_slice_in_dim(values, first_kv * HD, kv_local * HD, 1)
     key_all, value_all = (
-        lax.all_gather(key_local, "gx", axis=0, tiled=True),
+        exchange_gather(key_local, "gx", 0),
         lax.all_gather(value_local, "gx", axis=0, tiled=True),
     )
     total = key_all.shape[0]

time: 500 us -> 462 us (0.924)
  blocking collectives: 239 us -> 191 us
  starting transfers between devices: 31 us -> 41.1 us
    all_gather x1 -> x0, blocking collectives: 134 us -> none  [on_device(): lax.all_gather(key_local, 'gx', axis=0, tiled=True)]
    all_gather x1, blocking collectives: 48.7 us -> 135 us  [on_device(): lax.all_gather(value_local, 'gx', axis=0, tiled=True)]
    all_to_all x0 -> x1, starting transfers between devices: none -> 13.9 us  [exchange_gather(): return jnp.concatenate(lax.all_to_all(sent, mesh_axis, 0, 0), axis=d)]
  transfers between devices with their start and end apart: 5 -> 6, of which waited for: 2 -> 2; matrix products, arithmetic and copies ran while one was open for 5% -> 7% of each run, Pallas kernels for 0% -> 0%
where the time goes in v1:
time: 462 us; the launch traced here: 461 us
  blocking collectives  191 us (41%)
  waiting for transfers between devices  176 us (38%)
  starting transfers between devices  41.1 us (9%)
  local copies, waits for them, and re-layouts  17.7 us (4%)
  between operations  14.3 us (3%)
  matrix products  14 us (3%)
  other arithmetic  7.06 us (2%)
    all_gather x1, blocking collectives, on_device(): lax.all_gather(value_local, 'gx', axis=0, tiled=True)  135 us
    unnamed x3, waiting for transfers between devices  131 us
    psum x1, waiting for transfers between devices, on_device(): lax.psum((gate_terms, key_full, value_full), 'ta')  44.9 us
    psum x1, blocking collectives, on_device(): lax.psum((gate_terms, key_full, value_full), 'ta')  29.7 us
    all_gather x1, blocking collectives, on_device(): full_rows = lax.all_gather(picked, 'ta', axis=1, tiled=True)  26.4 us
    all_to_all x1, starting transfers between devices, exchange_gather(): return jnp.concatenate(lax.all_to_all(sent, mesh_axis, 0, 0), axis=d)  13.9 us
    all_to_all x1, starting transfers between devices, on_device(): lax.all_to_all(packed.astype(jnp.bfloat16).reshape(n_experts, cap, full_r...  10.5 us
  transfers between devices with their start and end apart: 6, of which 2 were waited for; matrix products, arithmetic and copies ran while one was open for 7% of the time, Pallas kernels for 0%

profile of v1, /device:TPU:2, one launch (start us, length us, event | category | flops | bytes accessed | tf_op | source)
XLA Modules:
  0.0 461.1 jit_solution(15133598699042790482)
XLA Ops:
  7.2 0.0 copy-start
  7.2 0.8 constant_dynamic-slice_fusion.1
  8.1 0.9 stack.2
  8.9 13.9 %all-to-all-start.3 = ((bf16[64,32,128]{2,1,0:T(8,128)(2,1)}), bf16[64,32,128]{2,1,0:T(8,128)(2,1)S(1)}, u32[]{:S(2)}, u32[]{:S(2)}) async-start(bf16[64,32,128]{2,1,0:T(8,128)(2,1)} %stack.2), calls=%async_computation.3 | async-start | bytes 1048576 | tf_op jit(solution)/shard_map/all_to_all | solution.py:13
  22.8 0.8 copy.53
  23.6 0.1 reshape.207
  23.6 0.0 copy-start.7
  23.7 0.1 eq.48
  23.7 0.7 compare_and_fusion
  24.4 0.6 reduce-window.6
  25.0 0.2 slice_reduce_fusion
  25.3 0.1 fusion.48
  25.4 0.1 reduce_sum.67
  25.5 0.6 gather_fusion
  26.2 0.1 broadcast_select_fusion
  26.2 26.4 %all_gather.6 = bf16[32,4096]{1,0:T(8,128)(2,1)S(1)} all-gather(bf16[32,512]{1,0:T(8,128)(2,1)S(1)} %broadcast_select_fusion), channel_id=1, replica_groups=mesh['gx'=64,'ta'=8] {'ta'}, dimensions={1}, use_global_device_ids=true | all-gather | bytes 294912 | tf_op jit(solution)/shard_map/all_gather | solution.py:38
  52.7 0.2 convert_reduce_fusion
  52.9 3.2 fusion
  56.2 10.5 %all-to-all-start.1 = ((bf16[64,8,4096]{2,1,0:T(8,128)(2,1)}), bf16[64,8,4096]{2,1,0:T(8,128)(2,1)}, u32[]{:S(2)}, u32[]{:S(2)}) async-start(bf16[64,8,4096]{2,1,0:T(8,128)(2,1)} %fusion), calls=%async_computation.1 | async-start | bytes 8388608 | tf_op jit(solution)/shard_map/all_to_all | solution.py:42
  66.7 0.0 reduce-scatter.4.cloned.1.call-start
  66.8 0.7 constant_dynamic-slice_fusion
  67.5 134.8 %all_gather.7 = bf16[2048,128]{1,0:T(8,128)(2,1)S(1)} all-gather(bf16[32,128]{1,0:T(8,128)(2,1)S(1)} %constant_dynamic-slice_fusion), channel_id=1, replica_groups=mesh['gx'=64,'ta'=8] {'gx'}, dimensions={0}, use_global_device_ids=true | all-gather | bytes 532480 | tf_op jit(solution)/shard_map/all_gather | solution.py:84
  202.2 0.1 iota_compare_fusion.2
  202.4 0.5 fusion.62
  202.9 0.0 copy-start.10
  202.9 0.4 fusion.9
  203.4 0.4 copy-done.10
  203.8 0.7 multiply_reduce_fusion
  204.4 0.6 fusion.18
  205.0 0.4 fusion.7
  205.4 0.6 convolution_bitcast_fusion.1
  206.0 1.4 pad_maximum_fusion
  207.4 3.0 copy.68
  210.4 0.0 reduce-scatter.4.cloned.1.call-update
  210.4 0.8 copy.56
  211.2 0.7 reshape.218
  211.9 0.7 multiply_add_fusion.1
  212.6 0.4 fusion.17
  213.1 0.6 copy.98
  213.7 3.8 fusion.31
  217.5 0.7 all_to_all.18
  218.2 8.5 %all-to-all-start.2 = ((f32[64,1,8]{2,1,0:T(1,128)}), f32[64,1,8]{2,1,0:T(1,128)S(1)}, u32[]{:S(2)}, u32[]{:S(2)}) async-start(f32[64,1,8]{2,1,0:T(1,128)} %bitcast.11), calls=%async_computation.2 | async-start | bytes 65536 | tf_op jit(solution)/shard_map/all_to_all | solution.py:69
  226.7 131.1 %reduce-scatter.4.cloned.1.call-done = f32[32,256]{1,0:T(8,128)} async-done(((f32[2048,256]{1,0:T(8,128)}), f32[32,256]{1,0:T(8,128)}) %reduce-scatter.4.cloned.1.call-update) | async-done | bytes 32784
  357.8 0.7 slice_dynamic-update-slice_fusion.1
  358.6 0.5 broadcast.114
  359.1 0.7 reduce.12
  359.8 0.1 broadcast_in_dim.79
  359.9 0.2 select_reduce_fusion
  360.2 0.7 convert_element_type.130
  360.9 8.1 %all-to-all-start = ((bf16[64,1,8]{2,1,0:T(2,128)(2,1)}), bf16[64,1,8]{2,1,0:T(2,128)(2,1)S(1)}, u32[]{:S(2)}, u32[]{:S(2)}) async-start(bf16[64,1,8]{2,1,0:T(2,128)(2,1)} %convert_element_type.130), calls=%async_computation | async-start | bytes 65536 | tf_op jit(solution)/shard_map/all_to_all | solution.py:49
  369.0 0.0 all-reduce.3.cloned.1.call-start
  369.1 0.7 slice_dynamic-update-slice_fusion
  369.8 0.6 copy-done.3
  370.4 0.0 all-reduce.3.cloned.1.call-update
  370.5 0.1 reshape.211
  370.5 29.7 %psum.21 = f32[32,8]{1,0:T(8,128)S(1)} all-reduce(f32[32,8]{1,0:T(8,128)S(1)} %reshape.211), channel_id=1, replica_groups=mesh['gx'=64,'ta'=8] {'ta'}, use_global_device_ids=true, to_apply=%region_7.8 | all-reduce | flops 256 | bytes 2048 | tf_op jit(solution)/shard_map/psum | solution.py:134
  400.2 0.7 copy.67
  400.9 0.1 convert_reduce_fusion.1
  401.0 0.1 reshape.219
  401.0 4.4 fusion.1
  405.4 0.9 fusion.41
  406.4 44.9 %all-reduce.3.cloned.1.call-done = (f32[32,512]{1,0:T(8,128)}, f32[32,512]{1,0:T(8,128)}) async-done(((f32[32,512]{1,0:T(8,128)}, f32[32,512]{1,0:T(8,128)}), (f32[32,512]{1,0:T(8,128)}, f32[32,512]{1,0:T(8,128)})) %all-reduce.3.cloned.1.call-update) | async-done | bytes 131088 | tf_op jit(solution)/shard_map/psum | solution.py:134
  451.3 1.5 copy.103
  452.8 1.5 copy.104
  (30 shorter events, 0.2 us)
Async XLA Ops:
  7.2 206.5 %copy-start = (bf16[1,192,4096]{2,1,0:T(8,128)(2,1)S(1)}, bf16[1,192,4096]{2,1,0:T(8,128)(2,1)}, u32[]{:S(2)}) copy-start(bf16[1,192,4096]{2,1,0:T(8,128)(2,1)} %param.15) | copy-start | bytes 4718596
  7.2 18.3 %copy-start.2 = (bf16[256,512]{1,0:T(8,128)(2,1)S(1)}, bf16[256,512]{1,0:T(8,128)(2,1)}, u32[]{:S(2)}) copy-start(bf16[256,512]{1,0:T(8,128)(2,1)} %param.11) | copy-start | bytes 786436
  8.9 47.2 %all-to-all-start.3 = ((bf16[64,32,128]{2,1,0:T(8,128)(2,1)}), bf16[64,32,128]{2,1,0:T(8,128)(2,1)S(1)}, u32[]{:S(2)}, u32[]{:S(2)}) async-start(bf16[64,32,128]{2,1,0:T(8,128)(2,1)} %stack.2), calls=%async_computation.3 | async-start | bytes 1048576 | tf_op jit(solution)/shard_map/all_to_all | solution.py:13
  23.6 2.5 copy-start.7
  25.4 0.8 copy-start.8
  56.2 146.2 %copy-start.1 = (bf16[32,1024]{1,0:T(8,128)(2,1)S(1)}, bf16[32,1024]{1,0:T(8,128)(2,1)}, u32[]{:S(2)}) copy-start(bf16[32,1024]{1,0:T(8,128)(2,1)} %param.18) | copy-start | bytes 196612
  56.2 157.5 %all-to-all-start.1 = ((bf16[64,8,4096]{2,1,0:T(8,128)(2,1)}), bf16[64,8,4096]{2,1,0:T(8,128)(2,1)}, u32[]{:S(2)}, u32[]{:S(2)}) async-start(bf16[64,8,4096]{2,1,0:T(8,128)(2,1)} %fusion), calls=%async_computation.1 | async-start | bytes 8388608 | tf_op jit(solution)/shard_map/all_to_all | solution.py:42
  66.7 291.1 %reduce-scatter.4.cloned.1.call-start = ((), (), s32[]{:S(2)}) async-start(), calls=%async_computation.5 | async-start | bytes 2129920
  202.9 0.8 copy-start.10
  210.4 3.3 copy-start.5
  210.4 3.3 copy-start.6
  213.7 146.2 %copy-start.9 = (f32[256]{0:T(256)S(1)}, f32[256]{0:T(256)}, u32[]{:S(2)}) copy-start(f32[256]{0:T(256)} %reshape.218) | copy-start | bytes 3076
  218.2 140.4 %all-to-all-start.2 = ((f32[64,1,8]{2,1,0:T(1,128)}), f32[64,1,8]{2,1,0:T(1,128)S(1)}, u32[]{:S(2)}, u32[]{:S(2)}) async-start(f32[64,1,8]{2,1,0:T(1,128)} %bitcast.11), calls=%async_computation.2 | async-start | bytes 65536 | tf_op jit(solution)/shard_map/all_to_all | solution.py:69
  358.6 11.2 %copy-start.4 = (f32[32,512]{1,0:T(8,128)}, f32[32,512]{1,0:T(8,128)S(1)}, u32[]{:S(2)}) copy-start(f32[32,512]{1,0:T(8,128)S(1)} %slice_dynamic-update-slice_fusion.1) | copy-start | bytes 196612
  360.9 40.0 %all-to-all-start = ((bf16[64,1,8]{2,1,0:T(2,128)(2,1)}), bf16[64,1,8]{2,1,0:T(2,128)(2,1)S(1)}, u32[]{:S(2)}, u32[]{:S(2)}) async-start(bf16[64,1,8]{2,1,0:T(2,128)(2,1)} %convert_element_type.130), calls=%async_computation | async-start | bytes 65536 | tf_op jit(solution)/shard_map/all_to_all | solution.py:49
  369.0 82.3 %all-reduce.3.cloned.1.call-start = ((), (), s32[]{:S(2)}) async-start(), calls=%async_computation.6 | async-start | bytes 262144 | tf_op jit(solution)/shard_map/psum | solution.py:134
  369.8 0.6 copy-start.3
Sparse Core Ops, SparseCore 0:
  210.5 147.2 reduce-scatter.3
  372.8 78.5 all-reduce.2
